TPU v7x, 256 devices: a whole 4x4x8 slice. The times are simulated.
256 devices in a mesh: seq: 32 (over y, z), tensor: 8 (over x, core).
Axes of the slice: x: 4, y: 4, z: 8, core: 2. Of those that a mesh axis runs over, the one named last changes fastest.
Arguments:
- state: bfloat16 [32768, 2048], P('seq', 'tensor'), may hold values from -20.5 to 20.5
- memory: bfloat16 [512, 2048], P('seq', 'tensor'), may hold values from -20.5 to 20.5
- w_query: bfloat16 [2048, 2048], P('seq', 'tensor'), may hold values from -0.1875 to 0.1875
- w_key: bfloat16 [2048, 2048], P('seq', 'tensor'), may hold values from -0.1875 to 0.1875
- w_value: bfloat16 [2048, 2048], P('seq', 'tensor'), may hold values from -0.125 to 0.125
- w_output: bfloat16 [2048, 2048], P('tensor', 'seq'), may hold values from -0.375 to 0.375
- norm_gain: float32 [2048], P('tensor'), may hold values from 0.1 to 1.9
- remaining: int32 [32768], P('seq'), may hold values from 0 to 3
- slot_home: int32 [512], replicated, may hold values from 0 to 31
Outputs:
- new_state: bfloat16 [32768, 2048], P('seq', 'tensor')
- new_memory: bfloat16 [512, 2048], P('seq', 'tensor')
Inputs may be any that keep to these rules, and one draw needn't show every extreme that they name: `remaining`: 0 means the token has halted.
All inputs are finite; a program needn't handle non-finite values.
Results may differ from a plain program's by a relative error of at most 0.014.
The roundings to bfloat16 on the way count: a program that leaves them out, or rounds other values in their place, can miss the bound.
Values may be sent and summed in bfloat16 or wider, within the bound.
No kernel may reach another device: no remote copies, remote signals or barrier semaphores. Data moves between devices by JAX's collectives and lax.ppermute only.
A program may use at most 128 MiB of HBM per device.

v0:
```python
import math
import jax
import jax.numpy as jnp
from jax import lax
from jax.sharding import PartitionSpec as P

D = 2048
H = 16
HD = 128
HALF = 256
QB = 512
EPS = 1e-05
MASKED = -1e30


def with_halo(array, sides, width):
    for axis, dim in sides:
        peers, length = (lax.axis_size(axis), array.shape[dim])
        up = [(i, (i + 1) % peers) for i in range(peers - 1)]
        down = [(j, i) for i, j in up]
        last = lax.slice_in_dim(array, length - width, length, axis=dim)
        initial = lax.slice_in_dim(array, 0, width, axis=dim)
        before = lax.ppermute(last, axis, up)
        after = lax.ppermute(initial, axis, down)
        array = jnp.concatenate([before, array, after], axis=dim)
    return array


def merged(part, axis, combine):
    gathered = jax.tree.map(lambda a: lax.all_gather(a, axis), part)

    def take(source):
        return jax.tree.map(lambda a: lax.dynamic_index_in_dim(a, source, 0, False), gathered)

    return lax.fori_loop(
        1, lax.axis_size(axis), lambda source, state: combine(state, take(source)), take(0)
    )


def head_slopes(first, amount):
    order = (first + jnp.arange(amount, dtype=jnp.int32)).astype(jnp.float32)
    return 0.25 * 8.0 ** (order / (H - 1))


def shards(state, memory, w_query, w_key, w_value, w_output, norm_gain, remaining, slot_home):
    tok_rows = state.shape[0]
    slot_rows = memory.shape[0]
    seq_count = lax.axis_size("seq")
    seq_place = lax.axis_index("seq")
    tensor_place = lax.axis_index("tensor")
    local_width = w_query.shape[1]
    local_heads = local_width // HD
    total_tokens = tok_rows * seq_count
    score_scale = 1.0 / math.sqrt(HD)
    distance_slopes = head_slopes(tensor_place * local_heads, local_heads)
    homes = slot_home.astype(jnp.float32)
    home_gap = jnp.abs(homes - seq_place.astype(jnp.float32))
    slot_bias = distance_slopes[:, None] * home_gap[None, :]
    state_full, memory_full = (
        lax.all_gather(state, "tensor", axis=1, tiled=True),
        lax.all_gather(memory, "tensor", axis=1, tiled=True),
    )
    rows_full = jnp.concatenate([state_full, memory_full], axis=0)
    pieces = (
        lax.all_gather(w_query, "seq", axis=0, tiled=True),
        lax.all_gather(w_key, "seq", axis=0, tiled=True),
        lax.all_gather(w_value, "seq", axis=0, tiled=True),
    )
    query_acc, key_acc, value_acc = tuple(
        (jnp.dot(rows_full, piece, preferred_element_type=jnp.float32) for piece in pieces)
    )
    query = query_acc.astype(jnp.bfloat16)
    keys = key_acc.astype(jnp.bfloat16)
    values = value_acc.astype(jnp.bfloat16)
    slot_heads = jnp.concatenate([query[tok_rows:], keys[tok_rows:], values[tok_rows:]], axis=1)
    all_slots = lax.all_gather(slot_heads, "seq", axis=0, tiled=True)
    memory_slot_query = all_slots[:, :local_width].reshape(-1, local_heads, HD)
    memory_slot_keys = all_slots[:, local_width : 2 * local_width].reshape(-1, local_heads, HD)
    memory_slot_values = all_slots[:, 2 * local_width :].reshape(-1, local_heads, HD)
    token_key_rows = keys[:tok_rows].reshape(tok_rows, local_heads, HD)
    token_value_rows = values[:tok_rows].reshape(tok_rows, local_heads, HD)
    keys_values = jnp.concatenate([keys[:tok_rows], values[:tok_rows]], axis=1)
    padded = with_halo(keys_values, (("seq", 0),), HALF)
    block = QB
    window_extent = block + 2 * HALF

    def one_block(number):
        start = number * block
        query_matrix = lax.dynamic_slice_in_dim(query, start, block, 0).reshape(
            block, local_heads, HD
        )
        near_rows = lax.dynamic_slice_in_dim(padded, start, window_extent, 0)
        near_keys = near_rows[:, :local_width].reshape(window_extent, local_heads, HD)
        near_values = near_rows[:, local_width:].reshape(window_extent, local_heads, HD)
        near = (
            jnp.einsum("qhd,khd->hqk", query_matrix, near_keys, preferred_element_type=jnp.float32)
            * score_scale
        )
        first = seq_place * tok_rows + start
        qpos = first + jnp.arange(block, dtype=jnp.int32)
        kpos = first - HALF + jnp.arange(window_extent, dtype=jnp.int32)
        valid = (
            (jnp.abs(qpos[:, None] - kpos[None, :]) <= HALF)
            & (kpos >= 0)[None, :]
            & (kpos < total_tokens)[None, :]
        )
        near = jnp.where(valid[None], near, MASKED)
        distant_mask = (
            jnp.einsum(
                "taw,caw->atc", query_matrix, memory_slot_keys, preferred_element_type=jnp.float32
            )
            * score_scale
            - slot_bias[:, None, :]
        )
        scores = jnp.concatenate([near, distant_mask], axis=2)
        top = jnp.max(scores, axis=2, keepdims=True)
        exponent_terms = jnp.exp(scores - top)
        total = jnp.sum(exponent_terms, axis=2)
        attention_probabilities = exponent_terms.astype(jnp.bfloat16)
        numer = jnp.einsum(
            "hqk,khd->qhd",
            attention_probabilities[:, :, :window_extent],
            near_values,
            preferred_element_type=jnp.float32,
        )
        numer = numer + jnp.einsum(
            "lse,elf->slf",
            attention_probabilities[:, :, window_extent:],
            memory_slot_values,
            preferred_element_type=jnp.float32,
        )
        return (
            (numer / jnp.transpose(total)[:, :, None])
            .astype(jnp.bfloat16)
            .reshape(block, local_width)
        )

    token_mix = lax.map(one_block, jnp.arange(tok_rows // block, dtype=jnp.int32)).reshape(
        tok_rows, local_width
    )
    unnormalized_scores = (
        jnp.einsum(
            "gki,pki->kgp", memory_slot_query, token_key_rows, preferred_element_type=jnp.float32
        )
        * score_scale
        - slot_bias[:, :, None]
    )
    local_top = jnp.max(unnormalized_scores, axis=2)
    exponent_terms = jnp.exp(unnormalized_scores - local_top[:, :, None])
    local_sum = jnp.transpose(jnp.sum(exponent_terms, axis=2))
    local_num = jnp.einsum(
        "xzg,gxw->zxw",
        exponent_terms.astype(jnp.bfloat16),
        token_value_rows,
        preferred_element_type=jnp.float32,
    )
    local_top = jnp.transpose(local_top)

    def combine(first_part, second_part):
        top = jnp.maximum(first_part[0], second_part[0])
        weight_first = jnp.exp(first_part[0] - top)
        weight_second = jnp.exp(second_part[0] - top)
        sums = weight_first * first_part[1] + weight_second * second_part[1]
        numers = (
            weight_first[:, :, None] * first_part[2] + weight_second[:, :, None] * second_part[2]
        )
        return (top, sums, numers)

    merged_parts = merged((local_top, local_sum, local_num), "seq", combine)
    own_sum = lax.dynamic_slice_in_dim(merged_parts[1], seq_place * slot_rows, slot_rows, 0)
    own_num = lax.dynamic_slice_in_dim(merged_parts[2], seq_place * slot_rows, slot_rows, 0)
    slot_mix = (own_num / own_sum[:, :, None]).astype(jnp.bfloat16).reshape(slot_rows, local_width)
    mixed = jnp.concatenate([token_mix, slot_mix], axis=0)
    partial_rows = jnp.dot(
        mixed,
        lax.all_gather(w_output, "seq", axis=1, tiled=True),
        preferred_element_type=jnp.float32,
    )
    summed = lax.psum_scatter(
        partial_rows.astype(jnp.bfloat16), "tensor", scatter_dimension=1, tiled=True
    ).astype(jnp.float32)
    residual = jnp.concatenate([state, memory], axis=0).astype(jnp.float32) + summed
    squares = lax.psum(jnp.sum(residual * residual, axis=1), "tensor")
    normed_rows = (residual * lax.rsqrt(squares / D + EPS)[:, None] * norm_gain[None, :]).astype(
        jnp.bfloat16
    )
    new_state = jnp.where((remaining > 0)[:, None], normed_rows[:tok_rows], state)
    new_memory = normed_rows[tok_rows:]
    return (new_state, new_memory)


def solution(mesh):
    placed = (
        P("seq", "tensor"),
        P("seq", "tensor"),
        P("seq", "tensor"),
        P("seq", "tensor"),
        P("seq", "tensor"),
        P("tensor", "seq"),
        P("tensor"),
        P("seq"),
        P(),
    )
    return jax.shard_map(
        shards,
        mesh=mesh,
        in_specs=placed,
        out_specs=(P("seq", "tensor"), P("seq", "tensor")),
        check_vma=False,
    )
```

profile of v0, /device:TPU:1, one launch (start us, length us, event | category | flops | bytes accessed | tf_op | source)
XLA Modules:
  0.0 714.2 jit_solution(8940133622111685820)
XLA Ops:
  10.7 16.0 %all_gather.40 = bf16[16,2048]{1,0:T(8,128)(2,1)S(1)} all-gather(bf16[16,256]{1,0:T(8,128)(2,1)} %param.14), channel_id=1, replica_groups=mesh['seq'=32,'tensor'=8] {'tensor'}, dimensions={1}, use_global_device_ids=true | all-gather | bytes 73728 | tf_op jit(solution)/shard_map/all_gather | solution.py:61
  26.8 25.3 %all-gather.10.cloned.1.call-done = bf16[1024,2048]{1,0:T(8,128)(2,1)} async-done(((bf16[1024,256]{1,0:T(8,128)(2,1)}), bf16[1024,2048]{1,0:T(8,128)(2,1)}) %all-gather.10.cloned.1.call-update) | async-done | bytes 4194320 | tf_op jit(solution)/shard_map/all_gather | solution.py:60
  52.1 4.7 constant_dynamic-update-slice_fusion.2
  57.4 69.1 %all-gather.14.cloned.1.call-done = bf16[2048,256]{1,0:T(8,128)(2,1)} async-done(((bf16[64,256]{1,0:T(8,128)(2,1)}), bf16[2048,256]{1,0:T(8,128)(2,1)}) %all-gather.14.cloned.1.call-update) | async-done | bytes 1048592 | tf_op jit(solution)/shard_map/all_gather | solution.py:67
  126.5 3.8 convolution_convert_fusion.2
  130.4 72.6 %all-gather.12.cloned.1.call-done = bf16[2048,256]{1,0:T(8,128)(2,1)} async-done(((bf16[64,256]{1,0:T(8,128)(2,1)}), bf16[2048,256]{1,0:T(8,128)(2,1)}) %all-gather.12.cloned.1.call-update) | async-done | bytes 1048592 | tf_op jit(solution)/shard_map/all_gather | solution.py:66
  203.0 3.8 convolution_convert_fusion.3
  206.9 72.4 %all-gather.16.cloned.1.call-done = bf16[2048,256]{1,0:T(8,128)(2,1)} async-done(((bf16[64,256]{1,0:T(8,128)(2,1)}), bf16[2048,256]{1,0:T(8,128)(2,1)}) %all-gather.16.cloned.1.call-update) | async-done | bytes 1048592 | tf_op jit(solution)/shard_map/all_gather | solution.py:65
  279.3 3.8 convolution_convert_fusion.1
  284.1 36.9 %all_gather.44 = bf16[512,768]{1,0:T(8,128)(2,1)S(1)} all-gather(bf16[16,768]{1,0:T(8,128)(2,1)S(1)} %pad_maximum_fusion.4), channel_id=1, replica_groups=mesh['seq'=32,'tensor'=8] {'seq'}, dimensions={0}, use_global_device_ids=true | all-gather | bytes 811008 | tf_op jit(solution)/shard_map/all_gather | solution.py:76
  321.9 1.9 copy-done
  323.9 2.0 fusion.26
  326.6 2.5 collective-permute-start
  329.1 1.3 collective-permute-start.1
  332.0 36.6 %all-gather = f32[16384,2]{0,1:T(2,128)S(1)} all-gather(f32[512,2]{0,1:T(2,128)S(1)} %bitcast.123), channel_id=2, replica_groups=mesh['seq'=32,'tensor'=8] {'seq'}, dimensions={0}, use_global_device_ids=true | all-gather | bytes 135168 | tf_op jit(solution)/shard_map/all_gather | solution.py:30
  368.6 3.3 fusion.23
  371.9 35.7 %all-gather.1 = f32[16384,2]{0,1:T(2,128)S(1)} all-gather(f32[512,2]{0,1:T(2,128)S(1)} %bitcast.126), channel_id=3, replica_groups=mesh['seq'=32,'tensor'=8] {'seq'}, dimensions={0}, use_global_device_ids=true | all-gather | bytes 135168 | tf_op jit(solution)/shard_map/all_gather | solution.py:30
  409.9 22.6 %while.33 = (s32[]{:T(128)}, bf16[2,512,256]{2,1,0:T(8,128)(2,1)}, s32[2]{0:T(128)}, bf16[1536,512]{1,0:T(8,128)(2,1)S(1)}, s32[]{:T(128)}, /*index=5*/bf16[1040...) while((s32[]{:T(128)}, bf16[2,512,256]{2,1,0:T(8,128)(2,1)}, ...), condition=%wide.region_4.5_spmd.clone, body=%wide.region_0.4_spmd.clone.sunk | while | flops 819334656 | bytes 41282024 | solution.py:138
  409.9 1.3 dynamic_slice.92
  414.8 1.5 fusion.86
  416.3 1.2 fusion.89
  417.6 1.2 fusion.90
  421.2 1.3 dynamic_slice.92
  426.1 1.5 fusion.86
  428.9 1.2 fusion.90
  432.4 48.4 %all-gather.20.cloned.1.call-done = f32[16384,2,128]{0,2,1:T(8,128)} async-done(((f32[512,2,128]{0,2,1:T(8,128)}), f32[16384,2,128]{0,2,1:T(8,128)}) %all-gather.20.cloned.1.call-update) | async-done | bytes 16777232 | tf_op jit(solution)/shard_map/all_gather | solution.py:30
  482.2 25.0 %copy.46 = f32[16384,2,128]{2,1,0:T(2,128)} copy(f32[16384,2,128]{0,2,1:T(8,128)} %all-gather.20.cloned.1.call-done) | data formatting | bytes 33554432 | tf_op jit(solution)/shard_map/while | solution.py:35
  507.1 140.4 %while.32 = (s32[]{:T(128)}, f32[512,2]{0,1:T(2,128)S(1)}, f32[512,2]{0,1:T(2,128)S(1)}, f32[512,2,128]{2,1,0:T(2,128)S(1)}, f32[32,512,2]{1,2,0:T(2,128)S(1)}, ...) while((s32[]{:T(128)}, f32[512,2]{0,1:T(2,128)S(1)}, ...), condition=%wide.region_8.9_spmd, body=%wide.region_7.8_spmd.sunk | while | flops 399365 | bytes 1630351 | solution.py:35
  508.2 3.5 fusion.77
  512.7 3.5 fusion.77
  517.3 3.5 fusion.77
  521.8 3.5 fusion.77
  526.3 3.5 fusion.77
  530.9 3.5 fusion.77
  535.4 3.5 fusion.77
  539.9 3.5 fusion.77
  544.5 3.5 fusion.77
  549.0 3.5 fusion.77
  553.5 3.5 fusion.77
  558.0 3.5 fusion.77
  562.5 3.5 fusion.77
  567.1 3.5 fusion.77
  571.6 3.5 fusion.77
  576.1 3.5 fusion.77
  580.7 3.5 fusion.77
  585.2 3.5 fusion.77
  589.7 3.5 fusion.77
  594.3 3.5 fusion.77
  598.8 3.5 fusion.77
  603.3 3.5 fusion.77
  607.8 3.5 fusion.77
  612.4 3.5 fusion.77
  616.9 3.5 fusion.77
  621.4 3.5 fusion.77
  626.0 3.5 fusion.77
  630.5 3.5 fusion.77
  635.0 3.5 fusion.77
  639.5 3.5 fusion.77
  644.1 3.5 fusion.77
  647.9 4.5 convolution_convert_fusion
  653.1 34.7 %reduce-scatter.2.cloned.1.call-done = bf16[1040,256]{1,0:T(8,128)(2,1)} async-done(((bf16[1040,2048]{1,0:T(8,128)(2,1)}), bf16[1040,256]{1,0:T(8,128)(2,1)}) %reduce-scatter.2.cloned.1.call-update) | async-done | bytes 532496 | tf_op jit(solution)/shard_map/reduce_scatter | solution.py:179
  687.8 1.3 multiply_reduce_fusion
  689.1 15.3 %psum.7 = f32[1040]{0:T(1024)S(1)} all-reduce(f32[1040]{0:T(1024)S(1)} %multiply_reduce_fusion), channel_id=1, replica_groups=mesh['seq'=32,'tensor'=8] {'tensor'}, use_global_device_ids=true, to_apply=%region_11.12 | all-reduce | flops 1040 | bytes 8320 | tf_op jit(solution)/shard_map/psum | solution.py:183
  704.5 1.3 multiply_convert_fusion
  (217 shorter events, 57.5 us)
Async XLA Ops:
  7.2 44.9 %all-gather.10.cloned.1.call-start = ((), (), s32[]{:S(2)}) async-start(), calls=%async_computation.1 | async-start | bytes 4718592 | tf_op jit(solution)/shard_map/all_gather | solution.py:60
  7.9 118.6 %all-gather.14.cloned.1.call-start = ((), (), s32[]{:S(2)}) async-start(), calls=%async_computation.3 | async-start | bytes 1081344 | tf_op jit(solution)/shard_map/all_gather | solution.py:67
  8.6 194.4 %all-gather.12.cloned.1.call-start = ((), (), s32[]{:S(2)}) async-start(), calls=%async_computation.2 | async-start | bytes 1081344 | tf_op jit(solution)/shard_map/all_gather | solution.py:66
  9.4 270.0 %all-gather.16.cloned.1.call-start = ((), (), s32[]{:S(2)}) async-start(), calls=%async_computation.4 | async-start | bytes 1081344 | tf_op jit(solution)/shard_map/all_gather | solution.py:65
  10.0 470.9 %all-gather.20.cloned.1.call-start = ((), (), s32[]{:S(2)}) async-start(), calls=%async_computation.7 | async-start | bytes 17301504 | tf_op jit(solution)/shard_map/all_gather | solution.py:30
  10.7 46.1 %copy-start.11 = (f32[512]{0:T(512)}, f32[512]{0:T(512)S(1)}, u32[]{:S(2)}) copy-start(f32[512]{0:T(512)S(1)} %subtract_abs_fusion) | copy-start | bytes 6148
  26.7 30.1 %copy-start.14 = (f32[2]{0:T(128)}, f32[2]{0:T(128)S(1)}, u32[]{:S(2)}) copy-start(f32[2]{0:T(128)S(1)} %power_multiply_fusion) | copy-start | bytes 28
  26.8 295.1 %copy-start.13 = (f32[2,512]{1,0:T(2,128)}, f32[2,512]{1,0:T(2,128)S(1)}, u32[]{:S(2)}) copy-start(f32[2,512]{1,0:T(2,128)S(1)} %broadcast_multiply_fusion.1) | copy-start | bytes 12292
  284.1 39.7 %copy-start.8 = (bf16[1024,256]{0,1:T(8,128)(2,1)S(1)}, bf16[1024,256]{0,1:T(8,128)(2,1)}, u32[]{:S(2)}) copy-start(bf16[1024,256]{0,1:T(8,128)(2,1)} %copy.45) | copy-start | bytes 1572868
  321.9 1.9 copy-start
  325.9 322.0 %all-gather.18.cloned.1.call-start = ((), (), s32[]{:S(2)}) async-start(), calls=%async_computation.5 | async-start | bytes 1081344 | tf_op jit(solution)/shard_map/all_gather | solution.py:176
  326.5 361.3 %reduce-scatter.2.cloned.1.call-start = ((), (), s32[]{:S(2)}) async-start(), calls=%async_computation.6 | async-start | bytes 4792320 | tf_op jit(solution)/shard_map/reduce_scatter | solution.py:179
  326.6 81.1 %collective-permute-start = (bf16[256,512]{1,0:T(8,128)(2,1)S(1)}, bf16[256,512]{1,0:T(8,128)(2,1)S(1)}, u32[]{:S(2)}, u32[]{:S(2)}) collective-permute-start(bf16[256,512]{1,0:T(8,128)(2,1)S(1)} %get-tuple-element.403), channel_id=1, source_target_pairs={{0,8},{8,16},{16,24},{24,32},{32,40},{40,48},{48,56},{56,64},{64,7... | collective-permute-start | bytes 786440 | tf_op jit(solution)/shard_map/ppermute | solution.py:23
  329.1 79.2 %collective-permute-start.1 = (bf16[256,512]{1,0:T(8,128)(2,1)S(1)}, bf16[256,512]{1,0:T(8,128)(2,1)}, u32[]{:S(2)}, u32[]{:S(2)}) collective-permute-start(bf16[256,512]{1,0:T(8,128)(2,1)S(1)} %get-tuple-element.404), channel_id=1, source_target_pairs={{8,0},{16,8},{24,16},{32,24},{40,32},{48,40},{56,48},{64,56},{72,6... | collective-permute-start | bytes 786440 | tf_op jit(solution)/shard_map/ppermute | solution.py:24
  407.6 0.7 copy-start.10
  409.9 2.9 copy-start.3
  417.5 1.3 copy-start.1
  417.6 2.1 copy-start.9
  418.8 1.5 copy-start.5
  418.8 2.3 copy-start.4
  420.3 0.8 copy-start.6
  421.1 2.9 copy-start.3
  428.8 1.3 copy-start.1
  428.8 2.1 copy-start.9
  430.1 1.5 copy-start.5
  430.1 2.3 copy-start.4
  431.6 0.8 copy-start.6
  507.1 140.7 %copy-start.7 = (bf16[2,512,256]{2,1,0:T(8,128)(2,1)S(1)}, bf16[2,512,256]{2,1,0:T(8,128)(2,1)}, u32[]{:S(2)}) copy-start(bf16[2,512,256]{2,1,0:T(8,128)(2,1)} %get-tuple-element.294) | copy-start | bytes 1572868
  652.4 0.7 copy-start.15
  652.4 35.4 %copy-start.2 = (bf16[1024,256]{1,0:T(8,128)(2,1)S(1)}, bf16[1024,256]{1,0:T(8,128)(2,1)}, u32[]{:S(2)}) copy-start(bf16[1024,256]{1,0:T(8,128)(2,1)} %param.13) | copy-start | bytes 1572868
  652.4 35.4 %copy-start.12 = (bf16[16,256]{1,0:T(8,128)(2,1)S(1)}, bf16[16,256]{1,0:T(8,128)(2,1)}, u32[]{:S(2)}) copy-start(bf16[16,256]{1,0:T(8,128)(2,1)} %param.14) | copy-start | bytes 24580
  652.4 52.0 %copy-start.16 = (f32[256]{0:T(256)S(1)}, f32[256]{0:T(256)}, u32[]{:S(2)}) copy-start(f32[256]{0:T(256)} %param.19) | copy-start | bytes 3076
Sparse Core Ops, SparseCore 0:
  9.8 42.2 all-gather.9
  54.7 71.8 all-gather.13
  129.1 73.8 all-gather.11
  205.5 73.8 all-gather.15
  326.0 154.7 all-gather.19
  483.3 68.5 all-gather.17
  652.5 35.1 reduce-scatter.1
where the time goes:
time: 718 us; the launch traced here: 714 us
  waiting for transfers between devices  326 us (45%)
  other arithmetic  144 us (20%)
  blocking collectives  141 us (20%)
  local copies, waits for them, and re-layouts  55.6 us (8%)
  matrix products  26.7 us (4%)
  between operations  14.4 us (2%)
    add x31, other arithmetic, combine(): weight_first[:, :, None] * first_part[2]  108 us
    all_gather x1, waiting for transfers between devices, shards(): lax.all_gather(w_key, 'seq', axis=0, tiled=True)  72.6 us
    all_gather x1, waiting for transfers between devices, shards(): lax.all_gather(w_query, 'seq', axis=0, tiled=True)  72.4 us
    all_gather x2, blocking collectives, merged(): gathered = jax.tree.map(lambda a: lax.all_gather(a, axis), part)  72.3 us
    all_gather x1, waiting for transfers between devices, shards(): lax.all_gather(w_value, 'seq', axis=0, tiled=True)  69.1 us
    all_gather x1, waiting for transfers between devices, merged(): gathered = jax.tree.map(lambda a: lax.all_gather(a, axis), part)  48.4 us
    all_gather x1, blocking collectives, shards(): all_slots = lax.all_gather(slot_heads, 'seq', axis=0, tiled=True)  36.9 us
    reduce_scatter x1, waiting for transfers between devices, shards(): lax.psum_scatter(partial_rows.astype(jnp.bfloat16), 'tensor', scatter_dim...  34.7 us
  transfers between devices with their start and end apart: 9, of which 6 were waited for; matrix products, arithmetic and copies ran while one was open for 29% of the time, Pallas kernels for 0%

commit v1 on v0

--- a/solution.py
+++ b/solution.py
@@ -63,7 +63,9 @@
     rows_full = jnp.concatenate([state_full, memory_full], axis=0)
     pieces = (
         lax.all_gather(w_query, "seq", axis=0, tiled=True),
-        lax.all_gather(w_key, "seq", axis=0, tiled=True),
+        jnp.concatenate(
+            lax.all_to_all(jnp.stack([w_key] * lax.axis_size("seq")), "seq", 0, 0), axis=0
+        ),
         lax.all_gather(w_value, "seq", axis=0, tiled=True),
     )
     query_acc, key_acc, value_acc = tuple(

time: 718 us -> 642 us (0.89)
  waiting for transfers between devices: 326 us -> 238 us
  starting transfers between devices: 4.04 us -> 16 us
    all_gather x1 -> x0, waiting for transfers between devices: 72.6 us -> none  [shards(): lax.all_gather(w_key, 'seq', axis=0, tiled=True)]
    all_to_all x0 -> x1, starting transfers between devices: none -> 12 us  [shards(): lax.all_to_all(jnp.stack([w_key] * lax.axis_size('seq')), 'seq', 0, 0)]
    all_gather x1, waiting for transfers between devices: 25.3 us -> 13.9 us  [shards(): lax.all_gather(state, 'tensor', axis=1, tiled=True)]
  transfers between devices with their start and end apart: 9 -> 9, of which waited for: 6 -> 5; matrix products, arithmetic and copies ran while one was open for 29% -> 32% of each run, Pallas kernels for 0% -> 0%
where the time goes in v1:
time: 642 us; the launch traced here: 638 us
  waiting for transfers between devices  238 us (37%)
  other arithmetic  144 us (22%)
  blocking collectives  139 us (22%)
  local copies, waits for them, and re-layouts  57.6 us (9%)
  matrix products  26.4 us (4%)
  starting transfers between devices  16 us (2%)
  between operations  14.4 us (2%)
    add x31, other arithmetic, combine(): weight_first[:, :, None] * first_part[2]  108 us
    all_gather x2, blocking collectives, merged(): gathered = jax.tree.map(lambda a: lax.all_gather(a, axis), part)  72.4 us
    all_gather x1, waiting for transfers between devices, shards(): lax.all_gather(w_value, 'seq', axis=0, tiled=True)  69.1 us
    all_gather x1, waiting for transfers between devices, shards(): lax.all_gather(w_query, 'seq', axis=0, tiled=True)  69 us
    all_gather x1, waiting for transfers between devices, merged(): gathered = jax.tree.map(lambda a: lax.all_gather(a, axis), part)  48.2 us
    all_gather x1, blocking collectives, shards(): all_slots = lax.all_gather(slot_heads, 'seq', axis=0, tiled=True)  36.9 us
    reduce_scatter x1, waiting for transfers between devices, shards(): lax.psum_scatter(partial_rows.astype(jnp.bfloat16), 'tensor', scatter_dim...  34.6 us
    while x2, local copies, waits for them, and re-layouts, merged(): lax.fori_loop(1, lax.axis_size(axis), lambda source, state: combine(state...  25.2 us
  transfers between devices with their start and end apart: 9, of which 5 were waited for; matrix products, arithmetic and copies ran while one was open for 32% of the time, Pallas kernels for 0%

profile of v1, /device:TPU:1, one launch (start us, length us, event | category | flops | bytes accessed | tf_op | source)
XLA Modules:
  0.0 637.9 jit_solution(4023884986396734685)
XLA Ops:
  8.6 1.9 stack.2
  10.5 12.0 %all-to-all-start = ((bf16[32,64,256]{2,1,0:T(8,128)(2,1)}), bf16[32,64,256]{2,1,0:T(8,128)(2,1)S(1)}, u32[]{:S(2)}, u32[]{:S(2)}) async-start(bf16[32,64,256]{2,1,0:T(8,128)(2,1)} %stack.2), calls=%async_computation | async-start | bytes 2097152 | tf_op jit(solution)/shard_map/all_to_all | solution.py:67
  24.0 14.2 %all_gather.37 = bf16[16,2048]{1,0:T(8,128)(2,1)S(1)} all-gather(bf16[16,256]{1,0:T(8,128)(2,1)} %param.14), channel_id=1, replica_groups=mesh['seq'=32,'tensor'=8] {'tensor'}, dimensions={1}, use_global_device_ids=true | all-gather | bytes 73728 | tf_op jit(solution)/shard_map/all_gather | solution.py:61
  38.3 13.9 %all-gather.9.cloned.1.call-done = bf16[1024,2048]{1,0:T(8,128)(2,1)} async-done(((bf16[1024,256]{1,0:T(8,128)(2,1)}), bf16[1024,2048]{1,0:T(8,128)(2,1)}) %all-gather.9.cloned.1.call-update) | async-done | bytes 4194320 | tf_op jit(solution)/shard_map/all_gather | solution.py:60
  52.3 4.7 constant_dynamic-update-slice_fusion.2
  57.6 69.1 %all-gather.11.cloned.1.call-done = bf16[2048,256]{1,0:T(8,128)(2,1)} async-done(((bf16[64,256]{1,0:T(8,128)(2,1)}), bf16[2048,256]{1,0:T(8,128)(2,1)}) %all-gather.11.cloned.1.call-update) | async-done | bytes 1048592 | tf_op jit(solution)/shard_map/all_gather | solution.py:69
  126.7 3.8 convolution_convert_fusion.2
  130.6 3.5 convolution_convert_fusion.3
  134.2 69.0 %all-gather.13.cloned.1.call-done = bf16[2048,256]{1,0:T(8,128)(2,1)} async-done(((bf16[64,256]{1,0:T(8,128)(2,1)}), bf16[2048,256]{1,0:T(8,128)(2,1)}) %all-gather.13.cloned.1.call-update) | async-done | bytes 1048592 | tf_op jit(solution)/shard_map/all_gather | solution.py:65
  203.2 3.8 convolution_convert_fusion.1
  208.0 36.9 %all_gather.40 = bf16[512,768]{1,0:T(8,128)(2,1)S(1)} all-gather(bf16[16,768]{1,0:T(8,128)(2,1)S(1)} %pad_maximum_fusion.4), channel_id=1, replica_groups=mesh['seq'=32,'tensor'=8] {'seq'}, dimensions={0}, use_global_device_ids=true | all-gather | bytes 811008 | tf_op jit(solution)/shard_map/all_gather | solution.py:78
  245.8 1.9 copy-done
  247.7 2.0 fusion.26
  250.5 2.5 collective-permute-start
  252.9 1.3 collective-permute-start.1
  255.8 36.7 %all-gather = f32[16384,2]{0,1:T(2,128)S(1)} all-gather(f32[512,2]{0,1:T(2,128)S(1)} %bitcast.125), channel_id=2, replica_groups=mesh['seq'=32,'tensor'=8] {'seq'}, dimensions={0}, use_global_device_ids=true | all-gather | bytes 135168 | tf_op jit(solution)/shard_map/all_gather | solution.py:30
  292.5 3.3 fusion.23
  295.8 35.7 %all-gather.1 = f32[16384,2]{0,1:T(2,128)S(1)} all-gather(f32[512,2]{0,1:T(2,128)S(1)} %bitcast.128), channel_id=3, replica_groups=mesh['seq'=32,'tensor'=8] {'seq'}, dimensions={0}, use_global_device_ids=true | all-gather | bytes 135168 | tf_op jit(solution)/shard_map/all_gather | solution.py:30
  333.7 22.7 %while.33 = (s32[]{:T(128)}, bf16[2,512,256]{2,1,0:T(8,128)(2,1)}, s32[2]{0:T(128)}, bf16[1536,512]{1,0:T(8,128)(2,1)S(1)}, s32[]{:T(128)}, /*index=5*/bf16[1040...) while((s32[]{:T(128)}, bf16[2,512,256]{2,1,0:T(8,128)(2,1)}, ...), condition=%wide.region_4.5_spmd.clone, body=%wide.region_0.4_spmd.clone.sunk | while | flops 819334656 | bytes 41282024 | solution.py:140
  333.7 1.3 dynamic_slice.92
  338.7 1.5 fusion.86
  341.5 1.2 fusion.90
  345.1 1.3 dynamic_slice.92
  350.1 1.5 fusion.86
  352.8 1.2 fusion.90
  356.4 48.2 %all-gather.17.cloned.1.call-done = f32[16384,2,128]{0,2,1:T(8,128)} async-done(((f32[512,2,128]{0,2,1:T(8,128)}), f32[16384,2,128]{0,2,1:T(8,128)}) %all-gather.17.cloned.1.call-update) | async-done | bytes 16777232 | tf_op jit(solution)/shard_map/all_gather | solution.py:30
  406.0 25.0 %copy.46 = f32[16384,2,128]{2,1,0:T(2,128)} copy(f32[16384,2,128]{0,2,1:T(8,128)} %all-gather.17.cloned.1.call-done) | data formatting | bytes 33554432 | tf_op jit(solution)/shard_map/while | solution.py:35
  430.9 140.4 %while.32 = (s32[]{:T(128)}, f32[512,2]{0,1:T(2,128)S(1)}, f32[512,2]{0,1:T(2,128)S(1)}, f32[512,2,128]{2,1,0:T(2,128)S(1)}, f32[32,512,2]{1,2,0:T(2,128)S(1)}, ...) while((s32[]{:T(128)}, f32[512,2]{0,1:T(2,128)S(1)}, ...), condition=%wide.region_8.9_spmd, body=%wide.region_7.8_spmd.sunk | while | flops 399365 | bytes 1630351 | solution.py:35
  432.0 3.5 fusion.77
  436.5 3.5 fusion.77
  441.1 3.5 fusion.77
  445.6 3.5 fusion.77
  450.1 3.5 fusion.77
  454.6 3.5 fusion.77
  459.2 3.5 fusion.77
  463.7 3.5 fusion.77
  468.2 3.5 fusion.77
  472.8 3.5 fusion.77
  477.3 3.5 fusion.77
  481.8 3.5 fusion.77
  486.4 3.5 fusion.77
  490.9 3.5 fusion.77
  495.4 3.5 fusion.77
  499.9 3.5 fusion.77
  504.5 3.5 fusion.77
  509.0 3.5 fusion.77
  513.5 3.5 fusion.77
  518.1 3.5 fusion.77
  522.6 3.5 fusion.77
  527.1 3.5 fusion.77
  531.6 3.5 fusion.77
  536.2 3.5 fusion.77
  540.7 3.5 fusion.77
  545.2 3.5 fusion.77
  549.7 3.5 fusion.77
  554.3 3.5 fusion.77
  558.8 3.5 fusion.77
  563.3 3.5 fusion.77
  567.9 3.5 fusion.77
  571.7 4.5 convolution_convert_fusion
  576.9 34.6 %reduce-scatter.2.cloned.1.call-done = bf16[1040,256]{1,0:T(8,128)(2,1)} async-done(((bf16[1040,2048]{1,0:T(8,128)(2,1)}), bf16[1040,256]{1,0:T(8,128)(2,1)}) %reduce-scatter.2.cloned.1.call-update) | async-done | bytes 532496 | tf_op jit(solution)/shard_map/reduce_scatter | solution.py:181
  611.5 1.3 multiply_reduce_fusion
  612.8 15.4 %psum.7 = f32[1040]{0:T(1024)S(1)} all-reduce(f32[1040]{0:T(1024)S(1)} %multiply_reduce_fusion), channel_id=1, replica_groups=mesh['seq'=32,'tensor'=8] {'tensor'}, use_global_device_ids=true, to_apply=%region_11.12 | all-reduce | flops 1040 | bytes 8320 | tf_op jit(solution)/shard_map/psum | solution.py:185
  628.2 1.3 multiply_convert_fusion
  (217 shorter events, 58.2 us)
Async XLA Ops:
  7.2 45.1 %all-gather.9.cloned.1.call-start = ((), (), s32[]{:S(2)}) async-start(), calls=%async_computation.2 | async-start | bytes 4718592 | tf_op jit(solution)/shard_map/all_gather | solution.py:60
  7.9 118.8 %all-gather.11.cloned.1.call-start = ((), (), s32[]{:S(2)}) async-start(), calls=%async_computation.3 | async-start | bytes 1081344 | tf_op jit(solution)/shard_map/all_gather | solution.py:69
  10.5 120.1 %all-to-all-start = ((bf16[32,64,256]{2,1,0:T(8,128)(2,1)}), bf16[32,64,256]{2,1,0:T(8,128)(2,1)S(1)}, u32[]{:S(2)}, u32[]{:S(2)}) async-start(bf16[32,64,256]{2,1,0:T(8,128)(2,1)} %stack.2), calls=%async_computation | async-start | bytes 2097152 | tf_op jit(solution)/shard_map/all_to_all | solution.py:67
  22.5 180.7 %all-gather.13.cloned.1.call-start = ((), (), s32[]{:S(2)}) async-start(), calls=%async_computation.4 | async-start | bytes 1081344 | tf_op jit(solution)/shard_map/all_gather | solution.py:65
  23.3 381.4 %all-gather.17.cloned.1.call-start = ((), (), s32[]{:S(2)}) async-start(), calls=%async_computation.7 | async-start | bytes 17301504 | tf_op jit(solution)/shard_map/all_gather | solution.py:30
  24.0 33.0 %copy-start.11 = (f32[512]{0:T(512)}, f32[512]{0:T(512)S(1)}, u32[]{:S(2)}) copy-start(f32[512]{0:T(512)S(1)} %subtract_abs_fusion) | copy-start | bytes 6148
  38.3 18.7 %copy-start.14 = (f32[2]{0:T(128)}, f32[2]{0:T(128)S(1)}, u32[]{:S(2)}) copy-start(f32[2]{0:T(128)S(1)} %power_multiply_fusion) | copy-start | bytes 28
  38.3 207.4 %copy-start.13 = (f32[2,512]{1,0:T(2,128)}, f32[2,512]{1,0:T(2,128)S(1)}, u32[]{:S(2)}) copy-start(f32[2,512]{1,0:T(2,128)S(1)} %broadcast_multiply_fusion.1) | copy-start | bytes 12292
  208.0 39.7 %copy-start.8 = (bf16[1024,256]{0,1:T(8,128)(2,1)S(1)}, bf16[1024,256]{0,1:T(8,128)(2,1)}, u32[]{:S(2)}) copy-start(bf16[1024,256]{0,1:T(8,128)(2,1)} %copy.45) | copy-start | bytes 1572868
  245.8 2.0 copy-start
  249.8 321.9 %all-gather.15.cloned.1.call-start = ((), (), s32[]{:S(2)}) async-start(), calls=%async_computation.5 | async-start | bytes 1081344 | tf_op jit(solution)/shard_map/all_gather | solution.py:178
  250.4 361.1 %reduce-scatter.2.cloned.1.call-start = ((), (), s32[]{:S(2)}) async-start(), calls=%async_computation.6 | async-start | bytes 4792320 | tf_op jit(solution)/shard_map/reduce_scatter | solution.py:181
  250.5 81.0 %collective-permute-start = (bf16[256,512]{1,0:T(8,128)(2,1)S(1)}, bf16[256,512]{1,0:T(8,128)(2,1)S(1)}, u32[]{:S(2)}, u32[]{:S(2)}) collective-permute-start(bf16[256,512]{1,0:T(8,128)(2,1)S(1)} %get-tuple-element.403), channel_id=1, source_target_pairs={{0,8},{8,16},{16,24},{24,32},{32,40},{40,48},{48,56},{56,64},{64,7... | collective-permute-start | bytes 786440 | tf_op jit(solution)/shard_map/ppermute | solution.py:23
  252.9 79.2 %collective-permute-start.1 = (bf16[256,512]{1,0:T(8,128)(2,1)S(1)}, bf16[256,512]{1,0:T(8,128)(2,1)}, u32[]{:S(2)}, u32[]{:S(2)}) collective-permute-start(bf16[256,512]{1,0:T(8,128)(2,1)S(1)} %get-tuple-element.404), channel_id=1, source_target_pairs={{8,0},{16,8},{24,16},{32,24},{40,32},{48,40},{56,48},{64,56},{72,6... | collective-permute-start | bytes 786440 | tf_op jit(solution)/shard_map/ppermute | solution.py:24
  331.5 0.6 copy-start.10
  333.7 2.9 copy-start.3
  341.5 1.3 copy-start.1
  341.5 2.1 copy-start.9
  342.7 1.5 copy-start.5
  342.7 2.3 copy-start.4
  344.2 0.8 copy-start.6
  345.1 2.9 copy-start.3
  352.8 1.3 copy-start.1
  352.8 2.1 copy-start.9
  354.1 1.5 copy-start.5
  354.1 2.3 copy-start.4
  355.6 0.8 copy-start.6
  430.9 140.7 %copy-start.7 = (bf16[2,512,256]{2,1,0:T(8,128)(2,1)S(1)}, bf16[2,512,256]{2,1,0:T(8,128)(2,1)}, u32[]{:S(2)}) copy-start(bf16[2,512,256]{2,1,0:T(8,128)(2,1)} %get-tuple-element.294) | copy-start | bytes 1572868
  576.2 0.7 copy-start.15
  576.2 35.3 %copy-start.2 = (bf16[1024,256]{1,0:T(8,128)(2,1)S(1)}, bf16[1024,256]{1,0:T(8,128)(2,1)}, u32[]{:S(2)}) copy-start(bf16[1024,256]{1,0:T(8,128)(2,1)} %param.13) | copy-start | bytes 1572868
  576.2 35.3 %copy-start.12 = (bf16[16,256]{1,0:T(8,128)(2,1)S(1)}, bf16[16,256]{1,0:T(8,128)(2,1)}, u32[]{:S(2)}) copy-start(bf16[16,256]{1,0:T(8,128)(2,1)} %param.14) | copy-start | bytes 24580
  576.2 52.0 %copy-start.16 = (f32[256]{0:T(256)S(1)}, f32[256]{0:T(256)}, u32[]{:S(2)}) copy-start(f32[256]{0:T(256)} %param.19) | copy-start | bytes 3076
Sparse Core Ops, SparseCore 0:
  9.8 42.4 all-gather.8
  54.8 71.8 all-gather.10
  129.3 73.8 all-gather.12
  249.9 154.7 all-gather.16
  407.1 68.5 all-gather.14
  576.4 35.1 reduce-scatter.1
